TPU v7x, 32 devices: a whole 2x2x4 slice. The times are simulated.
32 devices in a mesh: tab: 8 (over z, x), blk: 4 (over y, core).
Axes of the slice: x: 2, y: 2, z: 4, core: 2. Of those that a mesh axis runs over, the one named last changes fastest.
Arguments:
- tables: bfloat16 [64, 512, 768], P('tab', 'blk'), may hold values from -6 to 6
- lengths: int32 [64], P('tab'), may hold values from 60 to 512, as said below
- cotangent: bfloat16 [64, 512, 768], P('tab', 'blk'), may hold values from -6 to 6
- step_count: int32 [1], replicated, may hold values from 2 to 20
- w_qkv: float32 [768, 2304], P('tab'), may hold values from -0.21875 to 0.21875
- w_out: float32 [768, 768], P('tab'), may hold values from -3.5 to 3.5
- w_up: float32 [768, 3072], P('tab'), may hold values from -0.21875 to 0.21875
- w_down: float32 [3072, 768], P('tab'), may hold values from -0.109375 to 0.109375
- vectors: float32 [768, 12], P('tab')
- first_qkv: float32 [768, 2304], P('tab'), may hold values from -128 to 128
- first_out: float32 [768, 768], P('tab'), may hold values from -12 to 12
- first_up: float32 [768, 3072], P('tab'), may hold values from -80 to 80
- first_down: float32 [3072, 768], P('tab'), may hold values from -64 to 64
- first_vec: float32 [768, 12], P('tab'), may hold values from -128 to 128
- second_qkv: float32 [768, 2304], P('tab'), may hold values from 16.384 to 262.144
- second_out: float32 [768, 768], P('tab'), may hold values from 0.16384 to 2.62144
- second_up: float32 [768, 3072], P('tab'), may hold values from 8.192 to 131.072
- second_down: float32 [3072, 768], P('tab'), may hold values from 5.89824 to 95.0272
- second_vec: float32 [768, 12], P('tab'), may hold values from 16.384 to 262.144
Outputs:
- output: bfloat16 [64, 512, 768], P('tab', 'blk')
- grad_input: float32 [64, 512, 768], P('tab', 'blk')
- moment_qkv: float32 [768, 2304], P('tab')
- square_qkv: float32 [768, 2304], P('tab')
- master_qkv: float32 [768, 2304], P('tab')
- copy_qkv: bfloat16 [768, 2304], P('tab')
- moment_out: float32 [768, 768], P('tab')
- square_out: float32 [768, 768], P('tab')
- master_out: float32 [768, 768], P('tab')
- copy_out: bfloat16 [768, 768], P('tab')
- moment_up: float32 [768, 3072], P('tab')
- square_up: float32 [768, 3072], P('tab')
- master_up: float32 [768, 3072], P('tab')
- copy_up: bfloat16 [768, 3072], P('tab')
- moment_down: float32 [3072, 768], P('tab')
- square_down: float32 [3072, 768], P('tab')
- master_down: float32 [3072, 768], P('tab')
- copy_down: bfloat16 [3072, 768], P('tab')
- moment_vec: float32 [768, 12], P('tab')
- square_vec: float32 [768, 12], P('tab')
- master_vec: float32 [768, 12], P('tab')
- copy_vec: bfloat16 [768, 12], P('tab')
Inputs may be any that keep to these rules, and one draw needn't show every extreme that they name: `lengths`: positions from a table's length on are padding; some table has exactly 512 live tokens.
All inputs are finite; a program needn't handle non-finite values.
Results may differ from a plain program's by a relative error of at most 0.018.
Values may be sent and summed in bfloat16 or wider, within the bound.
A program may use at most 256 MiB of HBM per device.

v0:
```python
from functools import partial
import jax
import jax.numpy as jnp
from jax import lax
from jax.sharding import PartitionSpec as P

D = 768
H = 12
HD = 64
LEN = 512
EPS = 1e-06
NEGATIVE = -1e30
BETA_ONE = 0.9
BETA_TWO = 0.999
ADAM_EPS = 1e-08
DECAY = 0.01
RATES = (1.0, 15.0, 1.0, 0.5, 5.0)


def layer_norm(hidden, gain_vec, shift_vec):
    row_mean = jnp.mean(hidden, axis=-1, keepdims=True)
    centred = hidden - row_mean
    variance = jnp.mean(centred * centred, axis=-1, keepdims=True)
    return centred * lax.rsqrt(variance + EPS) * gain_vec + shift_vec


def inner(left, right):
    return lax.dot_general(
        left, right, (((0,), (0,)), ((), ())), preferred_element_type=jnp.float32
    )


def back_mul(left, right):
    return lax.dot_general(
        left, right, (((1,), (1,)), ((), ())), preferred_element_type=jnp.float32
    )


def adam(master, gradient, first_moment, second_moment, rate_now, step_float):
    moment_new = BETA_ONE * first_moment + (1.0 - BETA_ONE) * gradient
    square_new = BETA_TWO * second_moment + (1.0 - BETA_TWO) * gradient * gradient
    fix_one = 1.0 - jnp.power(BETA_ONE, step_float)
    fix_two = 1.0 - jnp.power(BETA_TWO, step_float)
    update = moment_new / fix_one / (jnp.sqrt(square_new / fix_two) + ADAM_EPS)
    master_new = master - rate_now * (update + DECAY * master)
    return (moment_new, square_new, master_new, master_new.astype(jnp.bfloat16))


def local(
    tables,
    lengths,
    cotangent,
    step_count,
    w_qkv,
    w_out,
    w_up,
    w_down,
    vectors,
    first_qkv,
    first_out,
    first_up,
    first_down,
    first_vec,
    second_qkv,
    second_out,
    second_up,
    second_down,
    second_vec,
):
    masters = (w_qkv, w_out, w_up, w_down, vectors)
    firsts = (first_qkv, first_out, first_up, first_down, first_vec)
    seconds = (second_qkv, second_out, second_up, second_down, second_vec)
    full_qkv, full_out, full_up, full_down, full_vec = (
        lax.all_gather(w_qkv.astype(jnp.bfloat16), "tab", axis=0, tiled=True),
        lax.all_gather(w_out.astype(jnp.bfloat16), "tab", axis=0, tiled=True),
        lax.all_gather(w_up.astype(jnp.bfloat16), "tab", axis=0, tiled=True),
        lax.all_gather(w_down.astype(jnp.bfloat16), "tab", axis=0, tiled=True),
        lax.all_gather(vectors.astype(jnp.bfloat16), "tab", axis=0, tiled=True),
    )
    vec_f = full_vec.astype(jnp.float32)
    bias_up = vec_f[:, 8:12].T.reshape(-1)
    table_count = tables.shape[0]
    local_len = tables.shape[1]
    scale_q = HD ** (-0.5)
    valid_keys = (
        lax.broadcasted_iota(jnp.int32, (table_count, 1, 1, LEN), 3) < lengths[:, None, None, None]
    )

    def score_block(query_h, key_h):
        raw_scores = (
            jnp.einsum("bqhd,bkhd->bhqk", query_h, key_h, preferred_element_type=jnp.float32)
            * scale_q
        )
        return jnp.where(valid_keys, raw_scores, NEGATIVE)

    tok_rows = tables.reshape(-1, D)
    proj_qkv = jnp.dot(tok_rows, full_qkv, preferred_element_type=jnp.float32)
    query_b = (proj_qkv[:, :D] + vec_f[:, 0]).astype(jnp.bfloat16)
    key_loc = proj_qkv[:, D : 2 * D].astype(jnp.bfloat16).reshape(table_count, local_len, D)
    value_loc = (
        (proj_qkv[:, 2 * D :] + vec_f[:, 1]).astype(jnp.bfloat16).reshape(table_count, local_len, D)
    )
    key_all, value_all = (
        lax.all_gather(key_loc, "blk", axis=1, tiled=True),
        lax.all_gather(value_loc, "blk", axis=1, tiled=True),
    )
    query_h = query_b.reshape(table_count, local_len, H, HD)
    key_h = key_all.reshape(table_count, LEN, H, HD)
    value_h = value_all.reshape(table_count, LEN, H, HD)
    scores = score_block(query_h, key_h)
    row_top = jnp.max(scores, axis=-1, keepdims=True)
    exp_scores = jnp.exp(scores - row_top)
    row_total = jnp.sum(exp_scores, axis=-1, keepdims=True)
    log_total = row_top + jnp.log(row_total)
    probs_b = (exp_scores / row_total).astype(jnp.bfloat16)
    mixed_heads = jnp.einsum(
        "bhqk,bkhd->bqhd", probs_b, value_h, preferred_element_type=jnp.float32
    )
    mixed_heads = mixed_heads.reshape(-1, D).astype(jnp.bfloat16)
    attn_out = jnp.dot(mixed_heads, full_out, preferred_element_type=jnp.float32) + vec_f[:, 2]
    normed_one, norm_one_back = jax.vjp(
        layer_norm, tok_rows.astype(jnp.float32) + attn_out, vec_f[:, 4], vec_f[:, 5]
    )
    normed_b = normed_one.astype(jnp.bfloat16)
    hidden = jnp.dot(normed_b, full_up, preferred_element_type=jnp.float32) + bias_up
    active, gelu_back = jax.vjp(partial(jax.nn.gelu, approximate=False), hidden)
    active_b = active.astype(jnp.bfloat16)
    branch = jnp.dot(active_b, full_down, preferred_element_type=jnp.float32) + vec_f[:, 3]
    result, norm_two_back = jax.vjp(layer_norm, normed_one + branch, vec_f[:, 6], vec_f[:, 7])
    output = result.astype(jnp.bfloat16).reshape(tables.shape)
    grad_out = cotangent.reshape(-1, D).astype(jnp.float32)
    grad_two, grad_g2, grad_c2 = norm_two_back(grad_out)
    grad_b2 = jnp.sum(grad_two, axis=0)
    branch_b = grad_two.astype(jnp.bfloat16)
    gw_down = inner(active_b, branch_b)
    grad_hidden = gelu_back(back_mul(branch_b, full_down))[0]
    grad_b1 = jnp.sum(grad_hidden, axis=0)
    hidden_b = grad_hidden.astype(jnp.bfloat16)
    gw_up = inner(normed_b, hidden_b)
    grad_one, grad_g1, grad_c1 = norm_one_back(grad_two + back_mul(hidden_b, full_up))
    grad_bo = jnp.sum(grad_one, axis=0)
    attn_b = grad_one.astype(jnp.bfloat16)
    gw_out = inner(mixed_heads, attn_b)
    grad_mixed = (
        back_mul(attn_b, full_out).astype(jnp.bfloat16).reshape(table_count, local_len, H, HD)
    )
    key_back, value_back = (
        lax.all_gather(key_loc, "blk", axis=1, tiled=True),
        lax.all_gather(value_loc, "blk", axis=1, tiled=True),
    )
    key_again = key_back.reshape(table_count, LEN, H, HD)
    value_again = value_back.reshape(table_count, LEN, H, HD)
    probs_again = jnp.exp(score_block(query_h, key_again) - log_total)
    grad_probs = jnp.einsum(
        "bqhd,bkhd->bhqk", grad_mixed, value_again, preferred_element_type=jnp.float32
    )
    row_dot = jnp.sum(grad_probs * probs_again, axis=-1, keepdims=True)
    grad_scores = (probs_again * (grad_probs - row_dot)).astype(jnp.bfloat16)
    grad_query = (
        jnp.einsum(
            "bhqk,bkhd->bqhd", grad_scores, key_again, preferred_element_type=jnp.float32
        ).reshape(-1, D)
        * scale_q
    )
    probs_again_b = probs_again.astype(jnp.bfloat16)
    part_key = (
        jnp.einsum(
            "bhqk,bqhd->bkhd", grad_scores, query_h, preferred_element_type=jnp.float32
        ).reshape(table_count, LEN, D)
        * scale_q
    )
    part_value = jnp.einsum(
        "bhqk,bqhd->bkhd", probs_again_b, grad_mixed, preferred_element_type=jnp.float32
    ).reshape(table_count, LEN, D)
    grad_key, grad_value = (
        lax.psum_scatter(
            part_key.astype(jnp.bfloat16), "blk", scatter_dimension=1, tiled=True
        ).astype(jnp.float32),
        lax.psum_scatter(
            part_value.astype(jnp.bfloat16), "blk", scatter_dimension=1, tiled=True
        ).astype(jnp.float32),
    )
    grad_key = grad_key.reshape(-1, D)
    grad_value = grad_value.reshape(-1, D)
    grad_bq = jnp.sum(grad_query, axis=0)
    grad_bv = jnp.sum(grad_value, axis=0)
    grad_qkv = jnp.concatenate([grad_query, grad_key, grad_value], axis=1).astype(jnp.bfloat16)
    gw_qkv = inner(tok_rows, grad_qkv)
    grad_input = grad_one + back_mul(grad_qkv, full_qkv)
    gw_vec = jnp.concatenate(
        [
            jnp.stack(
                [grad_bq, grad_bv, grad_bo, grad_b2, grad_g1, grad_c1, grad_g2, grad_c2], axis=1
            ),
            grad_b1.reshape(4, D).T,
        ],
        axis=1,
    )
    share_qkv, share_out, share_up, share_down, share_vec = (
        lax.psum_scatter(gw_qkv, "tab", scatter_dimension=0, tiled=True),
        lax.psum_scatter(gw_out, "tab", scatter_dimension=0, tiled=True),
        lax.psum_scatter(gw_up, "tab", scatter_dimension=0, tiled=True),
        lax.psum_scatter(gw_down, "tab", scatter_dimension=0, tiled=True),
        lax.psum_scatter(gw_vec, "tab", scatter_dimension=0, tiled=True),
    )
    shares = (
        lax.psum(share_qkv.astype(jnp.bfloat16), "blk").astype(jnp.float32),
        lax.psum(share_out.astype(jnp.bfloat16), "blk").astype(jnp.float32),
        lax.psum(share_up.astype(jnp.bfloat16), "blk").astype(jnp.float32),
        lax.psum(share_down.astype(jnp.bfloat16), "blk").astype(jnp.float32),
        lax.psum(share_vec.astype(jnp.bfloat16), "blk").astype(jnp.float32),
    )
    step_float = step_count[0].astype(jnp.float32)
    results = [output, grad_input.reshape(tables.shape)]
    for position in range(5):
        results.extend(
            adam(
                masters[position],
                shares[position],
                firsts[position],
                seconds[position],
                RATES[position],
                step_float,
            )
        )
    return tuple(results)


def solution(mesh):
    return jax.shard_map(
        local,
        mesh=mesh,
        in_specs=(
            P("tab", "blk", None),
            P("tab"),
            P("tab", "blk", None),
            P(),
            P("tab", None),
            P("tab", None),
            P("tab", None),
            P("tab", None),
            P("tab", None),
            P("tab", None),
            P("tab", None),
            P("tab", None),
            P("tab", None),
            P("tab", None),
            P("tab", None),
            P("tab", None),
            P("tab", None),
            P("tab", None),
            P("tab", None),
        ),
        out_specs=(
            P("tab", "blk", None),
            P("tab", "blk", None),
            P("tab", None),
            P("tab", None),
            P("tab", None),
            P("tab", None),
            P("tab", None),
            P("tab", None),
            P("tab", None),
            P("tab", None),
            P("tab", None),
            P("tab", None),
            P("tab", None),
            P("tab", None),
            P("tab", None),
            P("tab", None),
            P("tab", None),
            P("tab", None),
            P("tab", None),
            P("tab", None),
            P("tab", None),
            P("tab", None),
        ),
        check_vma=False,
    )
```

profile of v0, /device:TPU:0, one launch (start us, length us, event | category | flops | bytes accessed | tf_op | source)
XLA Modules:
  0.0 1251.9 jit_solution(16198308453331200462)
XLA Ops:
  9.3 68.8 %all-gather.8.cloned.1.call-done = bf16[768,2304]{1,0:T(8,128)(2,1)} async-done(((bf16[96,2304]{1,0:T(8,128)(2,1)}), bf16[768,2304]{1,0:T(8,128)(2,1)}) %all-gather.8.cloned.1.call-update) | async-done | bytes 3538960 | tf_op jit(solution)/shard_map/all_gather | solution.py:74
  78.1 6.3 fusion.87
  84.4 3.6 copy-done.9
  89.4 30.6 %all-gather = bf16[8,96,12]{1,2,0:T(8,128)(2,1)S(1)} all-gather(bf16[1,96,12]{1,2,0:T(8,128)(2,1)S(1)} %convert_bitcast_fusion), channel_id=1, replica_groups=mesh['tab'=8,'blk'=4] {'tab'}, dimensions={0}, use_global_device_ids=true | all-gather | bytes 20736 | tf_op jit(solution)/shard_map/all_gather | solution.py:78
  120.8 4.7 fusion.16
  131.0 3.6 all-gather.12.cloned.1.call-done
  134.6 8.6 copy.104
  143.3 12.9 %fusion.12 = (f32[8,12,128]{2,1,0:T(8,128)S(1)}, f32[8,12,128,512]{3,2,1,0:T(8,128)}) fusion(pred[8,512]{1,0:T(8,128)(4,1)S(1)} %iota_compare_fusion, bf16[8,512,12,64]{1,3,2,0:T(8,128)(2,1)} %bitcast.94, bf16[8,128,12,64]{1,0,3,2:T(8,128)(2,1)S(1)} %bitcast.99), kind=kOutput, calls=%fused_computation.29 | convolution fusion | flops 824168448 | bytes 33083392 | tf_op jit(solution)/shard_map/bqhd,bkhd->bhqk/dot_general | solution.py:91
  156.1 11.6 fusion
  168.4 14.7 %all-gather.10.cloned.1.call-done = bf16[8,512,768]{2,1,0:T(8,128)(2,1)} async-done(((bf16[8,128,768]{2,1,0:T(8,128)(2,1)}), bf16[8,512,768]{2,1,0:T(8,128)(2,1)}) %all-gather.10.cloned.1.call-update) | async-done | bytes 6291472 | tf_op jit(solution)/shard_map/all_gather | solution.py:105
  183.1 8.6 copy.102
  191.8 13.4 %fusion.35 = bf16[8,128,12,64]{1,3,2,0:T(8,128)(2,1)S(1)} fusion(bf16[8,512,12,64]{1,3,2,0:T(8,128)(2,1)} %bitcast.97, f32[8,12,128]{2,1,0:T(8,128)S(1)} %fusion, f32[8,12,128]{2,1,0:T(8,128)S(1)} %get-tuple-element.136, f32[8,12,128,512]{3,2,1,0:T(8,128)} %get-tuple-element.137, pred[8,512]{1,0:T(8,128)(4,1)S(1)} %iota_compare_fusion), kind=kOutput, calls=%fused_computation.79 | convolution fusion | flops 837550080 | bytes 33132544 | tf_op jit(solution)/shard_map/bhqk,bkhd->bqhd/dot_general | solution.py:116
  207.6 19.3 %all-gather.14.cloned.1.call-done = bf16[768,768]{1,0:T(8,128)(2,1)} async-done(((bf16[96,768]{1,0:T(8,128)(2,1)}), bf16[768,768]{1,0:T(8,128)(2,1)}) %all-gather.14.cloned.1.call-update) | async-done | bytes 1179664 | tf_op jit(solution)/shard_map/all_gather | solution.py:75
  226.9 3.9 fusion.84
  231.3 76.3 %all-gather.16.cloned.1.call-done = bf16[768,3072]{1,0:T(8,128)(2,1)} async-done(((bf16[96,3072]{1,0:T(8,128)(2,1)}), bf16[768,3072]{1,0:T(8,128)(2,1)}) %all-gather.16.cloned.1.call-update) | async-done | bytes 4718608 | tf_op jit(solution)/shard_map/all_gather | solution.py:76
  307.6 36.0 %multiply_convert_fusion.2 = (bf16[1024,3072]{1,0:T(8,128)(2,1)}, f32[1024,3072]{1,0:T(8,128)}, f32[1024,3072]{1,0:T(8,128)}) fusion(f32[3072]{0:T(1024)S(1)} %add.223, bf16[768,3072]{1,0:T(8,128)(2,1)} %all-gather.16.cloned.1.call-done, f32[1024,768]{1,0:T(8,128)S(1)} %get-tuple-element.139, f32[768]{0:T(1024)S(1)} %get-tuple-element.96, ...), kind=kOutput, calls=%fused_computation.14 | convolution fusion | flops 5043388416 | bytes 39348224 | tf_op jit(solution)/shard_map/dot_general | solution.py:125
  343.6 44.3 %all-gather.18.cloned.1.call-done = bf16[3072,768]{1,0:T(8,128)(2,1)} async-done(((bf16[384,768]{1,0:T(8,128)(2,1)}), bf16[3072,768]{1,0:T(8,128)(2,1)}) %all-gather.18.cloned.1.call-update) | async-done | bytes 4718608 | tf_op jit(solution)/shard_map/all_gather | solution.py:77
  387.9 8.8 fusion.85
  399.9 3.1 fusion.82
  403.0 19.2 %fusion.86 = (f32[3072]{0:T(1024)S(1)}, bf16[1024,3072]{1,0:T(8,128)(2,1)}) fusion(f32[1024,3072]{1,0:T(8,128)} %get-tuple-element.130, bf16[3072,768]{1,0:T(8,128)(2,1)} %all-gather.18.cloned.1.call-done, f32[1024,768]{1,0:T(8,128)} %get-tuple-element.128, f32[1024]{0:T(1024)S(1)} %negate_multiply_fusion.2, f32[1024,3072]{1,0:T(8,128)} %get-tuple-element.140, ...), kind=kOutput, calls=%fused_computation.151 | convolution fusion | flops 4883739648 | bytes 39350272 | tf_op jit(solution)/shard_map/dot_general | solution.py:34
  422.2 10.0 multiply_reduce_fusion.1
  435.3 2.7 convolution_convert_fusion
  438.0 2.6 copy.107
  442.5 13.1 %fusion.13 = bf16[8,12,64,512]{3,2,1,0:T(8,128)(2,1)} fusion(f32[8,12,128]{2,1,0:T(8,128)S(1)} %copy-done.24, f32[8,12,128,512]{3,2,1,0:T(8,128)} %get-tuple-element.137, pred[8,512]{1,0:T(8,128)(4,1)S(1)} %copy-done.26, bf16[8,128,12,64]{1,0,3,2:T(8,128)(2,1)S(1)} %bitcast.108), kind=kOutput, calls=%fused_computation.34 | convolution fusion | flops 833617920 | bytes 33083392 | tf_op jit(solution)/shard_map/bhqk,bqhd->bkhd/dot_general | solution.py:172
  455.6 8.7 copy.113
  464.3 24.1 %multiply_reduce_fusion = (f32[8,12,128]{2,1,0:T(8,128)S(1)}, f32[8,12,128,512]{3,2,1,0:T(8,128)}) fusion(f32[8,12,128]{2,1,0:T(8,128)S(1)} %copy-done.24, f32[8,12,128,512]{3,2,1,0:T(8,128)} %get-tuple-element.137, pred[8,512]{1,0:T(8,128)(4,1)S(1)} %copy-done.26, bf16[8,512,12,64]{1,3,2,0:T(8,128)(2,1)} %bitcast.98, bf16[8,128,12,64]{1,0,3,2:T(8,128)(2,1)} %bitcast.109), kind=kOutput, calls=%fused_computation.1 | convolution fusion | flops 836751360 | bytes 58298368 | tf_op jit(solution)/shard_map/bqhd,bkhd->bhqk/dot_general | solution.py:154
  488.5 17.0 %multiply_convert_fusion = bf16[8,12,128,512]{3,2,1,0:T(8,128)(2,1)S(1)} fusion(f32[8,12,128,512]{3,2,1,0:T(8,128)} %get-tuple-element.145, f32[8,12,128]{2,1,0:T(8,128)S(1)} %get-tuple-element.144, f32[8,12,128]{2,1,0:T(8,128)S(1)} %copy-done.24, f32[8,12,128,512]{3,2,1,0:T(8,128)} %get-tuple-element.137, pred[8,512]{1,0:T(8,128)(4,1)S(1)} %copy-done.26), kind=kLoop, calls=%fused_computation | loop fusion | flops 37748736 | bytes 63016960 | tf_op jit(solution)/shard_map/convert_element_type | solution.py:158
  505.5 4.2 multiply_convert_fusion.1
  511.9 8.7 copy.111
  520.7 5.4 fusion.32
  526.2 10.8 fusion.22
  538.9 10.8 fusion.62
  550.0 10.8 multiply_reduce_fusion.5
  564.9 18.2 %reduce-scatter.12.cloned.1.call-done = bf16[8,128,768]{2,1,0:T(8,128)(2,1)} async-done(((bf16[8,512,768]{2,1,0:T(8,128)(2,1)}), bf16[8,128,768]{2,1,0:T(8,128)(2,1)}) %reduce-scatter.12.cloned.1.call-update) | async-done | bytes 1572880 | tf_op jit(solution)/shard_map/reduce_scatter | solution.py:176
  583.1 2.6 copy.114
  585.7 8.7 convolution_bitcast_fusion
  594.4 8.0 copy.117
  611.2 45.1 %reduce-scatter.16.cloned.1.call-done = f32[96,768]{1,0:T(8,128)} async-done(((f32[768,768]{1,0:T(8,128)}), f32[96,768]{1,0:T(8,128)}) %reduce-scatter.16.cloned.1.call-update) | async-done | bytes 294928 | tf_op jit(solution)/shard_map/reduce_scatter | solution.py:201
  657.9 163.1 %reduce-scatter.18.cloned.1.call-done = f32[96,3072]{1,0:T(8,128)} async-done(((f32[768,3072]{1,0:T(8,128)}), f32[96,3072]{1,0:T(8,128)}) %reduce-scatter.18.cloned.1.call-update) | async-done | bytes 1179664 | tf_op jit(solution)/shard_map/reduce_scatter | solution.py:202
  823.2 162.7 %reduce-scatter.20.cloned.1.call-done = f32[384,768]{1,0:T(8,128)} async-done(((f32[3072,768]{1,0:T(8,128)}), f32[384,768]{1,0:T(8,128)}) %reduce-scatter.20.cloned.1.call-update) | async-done | bytes 1179664 | tf_op jit(solution)/shard_map/reduce_scatter | solution.py:203
  988.0 130.0 %reduce-scatter.22.cloned.1.call-done = f32[96,2304]{1,0:T(8,128)} async-done(((f32[768,2304]{1,0:T(8,128)}), f32[96,2304]{1,0:T(8,128)}) %reduce-scatter.22.cloned.1.call-update) | async-done | bytes 884752 | tf_op jit(solution)/shard_map/reduce_scatter | solution.py:200
  1120.2 9.3 add_add_fusion.4
  1129.4 53.9 %reduce-scatter.24.cloned.1.call-done = f32[96,12]{1,0:T(8,128)} async-done(((f32[768,12]{1,0:T(8,128)}), f32[96,12]{1,0:T(8,128)}) %reduce-scatter.24.cloned.1.call-update) | async-done | bytes 4624
  1184.2 5.7 psum.39
  1190.5 42.2 %all-reduce.3.cloned.1.call-done = (bf16[96,2304]{1,0:T(8,128)(2,1)}, bf16[96,768]{1,0:T(8,128)(2,1)}, bf16[96,3072]{1,0:T(8,128)(2,1)}, bf16[384,768]{1,0:T(8,128)(2,1)}) async-done(((bf16[96,2304]{1,0:T(8,128)(2,1)}, bf16[96,768]{1,0:T(8,128)(2,1)}, bf16[96,3072]{1,0:T(8,128)(2,1)}, bf16[384,768]{1,0:T(8,128)(2,1)}), (bf16[96,2304]{1,0:T(8,128)(2,1)}, bf16[96,768]{1,0:T(8,128)(2,1)}, ...) | async-done | bytes 1769488 | tf_op jit(solution)/shard_map/psum | solution.py:207
  1234.9 4.0 fusion.78
  1239.0 2.5 fusion.72
  1242.5 2.6 fusion.69
  (156 shorter events, 50.5 us)
Async XLA Ops:
  7.2 70.9 %all-gather.8.cloned.1.call-start = ((), (), s32[]{:S(2)}) async-start(), calls=%async_computation.7 | async-start | bytes 3981312 | tf_op jit(solution)/shard_map/all_gather | solution.py:74
  9.2 125.4 %all-gather.12.cloned.1.call-start = ((), (), s32[]{:S(2)}) async-start(), calls=%async_computation.9 | async-start | bytes 7864320 | tf_op jit(solution)/shard_map/all_gather | solution.py:104
  84.4 3.6 copy-start.9
  89.4 93.8 %all-gather.10.cloned.1.call-start = ((), (), s32[]{:S(2)}) async-start(), calls=%async_computation.8 | async-start | bytes 7864320 | tf_op jit(solution)/shard_map/all_gather | solution.py:105
  120.8 4.8 copy-start.20
  120.8 5.5 copy-start.11
  125.5 4.2 copy-start.35
  125.5 101.4 %all-gather.14.cloned.1.call-start = ((), (), s32[]{:S(2)}) async-start(), calls=%async_computation.10 | async-start | bytes 1327104 | tf_op jit(solution)/shard_map/all_gather | solution.py:75
  126.2 181.3 %all-gather.16.cloned.1.call-start = ((), (), s32[]{:S(2)}) async-start(), calls=%async_computation.11 | async-start | bytes 5308416 | tf_op jit(solution)/shard_map/all_gather | solution.py:76
  127.2 260.7 %all-gather.18.cloned.1.call-start = ((), (), s32[]{:S(2)}) async-start(), calls=%async_computation.12 | async-start | bytes 5308416 | tf_op jit(solution)/shard_map/all_gather | solution.py:77
  129.4 433.2 %reduce-scatter.14.cloned.1.call-start = ((), (), s32[]{:S(2)}) async-start(), calls=%async_computation.14 | async-start | bytes 7864320 | tf_op jit(solution)/shard_map/reduce_scatter | solution.py:179
  129.7 62.0 %copy-start.25 = (pred[8,512]{1,0:T(8,128)(4,1)}, pred[8,512]{1,0:T(8,128)(4,1)S(1)}, u32[]{:S(2)}) copy-start(pred[8,512]{1,0:T(8,128)(4,1)S(1)} %iota_compare_fusion) | copy-start | bytes 12292
  131.0 12.3 copy-start.1
  307.6 80.3 %copy-start.34 = (f32[768]{0:T(1024)S(1)}, f32[768]{0:T(1024)}, u32[]{:S(2)}) copy-start(f32[768]{0:T(1024)} %get-tuple-element.95) | copy-start | bytes 9220
  397.3 2.7 copy-start.30
  432.2 3.1 copy-start.36
  433.7 1.6 copy-start.5
  438.0 4.5 copy-start.24
  438.0 4.5 copy-start.26
  442.4 13.1 %copy-start.10 = (bf16[96,8,8,128]{3,2,1,0:T(8,128)(2,1)}, bf16[96,8,8,128]{3,2,1,0:T(8,128)(2,1)S(1)}, u32[]{:S(2)}) copy-start(bf16[96,8,8,128]{3,2,1,0:T(8,128)(2,1)S(1)} %copy.123) | copy-start | bytes 4718596
  464.3 118.8 %reduce-scatter.12.cloned.1.call-start = ((), (), s32[]{:S(2)}) async-start(), calls=%async_computation.13 | async-start | bytes 7864320 | tf_op jit(solution)/shard_map/reduce_scatter | solution.py:176
  488.5 17.1 %copy-start.2 = (bf16[96,8,8,128]{3,2,1,0:T(8,128)(2,1)S(1)}, bf16[96,8,8,128]{3,2,1,0:T(8,128)(2,1)}, u32[]{:S(2)}) copy-start(bf16[96,8,8,128]{3,2,1,0:T(8,128)(2,1)} %copy-done.1) | copy-start | bytes 4718596
  505.5 6.4 copy-start
  520.7 135.6 %reduce-scatter.16.cloned.1.call-start = ((), (), s32[]{:S(2)}) async-start(), calls=%async_computation.15 | async-start | bytes 2654208 | tf_op jit(solution)/shard_map/reduce_scatter | solution.py:201
  526.1 294.9 %reduce-scatter.18.cloned.1.call-start = ((), (), s32[]{:S(2)}) async-start(), calls=%async_computation.16 | async-start | bytes 10616832 | tf_op jit(solution)/shard_map/reduce_scatter | solution.py:202
  537.0 2.0 copy-start.7
  537.0 448.9 %reduce-scatter.20.cloned.1.call-start = ((), (), s32[]{:S(2)}) async-start(), calls=%async_computation.17 | async-start | bytes 10616832 | tf_op jit(solution)/shard_map/reduce_scatter | solution.py:203
  549.8 568.3 %reduce-scatter.22.cloned.1.call-start = ((), (), s32[]{:S(2)}) async-start(), calls=%async_computation.18 | async-start | bytes 7962624 | tf_op jit(solution)/shard_map/reduce_scatter | solution.py:200
  562.6 23.2 %copy-start.14 = (bf16[96,8,8,128]{3,1,2,0:T(8,128)(2,1)}, bf16[96,8,8,128]{3,1,2,0:T(8,128)(2,1)S(1)}, u32[]{:S(2)}) copy-start(bf16[96,8,8,128]{3,1,2,0:T(8,128)(2,1)S(1)} %copy.149) | copy-start | bytes 4718596
  564.9 29.5 %copy-start.15 = (bf16[1024,768]{0,1:T(8,128)(2,1)}, bf16[1024,768]{0,1:T(8,128)(2,1)S(1)}, u32[]{:S(2)}) copy-start(bf16[1024,768]{0,1:T(8,128)(2,1)S(1)} %copy.115) | copy-start | bytes 4718596
  602.5 1.4 copy-start.4
  602.5 1.7 copy-start.31
  602.5 580.8 %reduce-scatter.24.cloned.1.call-start = ((), (), s32[]{:S(2)}) async-start(), calls=%async_computation.19 | async-start | bytes 442368
  604.2 2.9 copy-start.8
  610.2 622.5 %all-reduce.3.cloned.1.call-start = ((), (), s32[]{:S(2)}) async-start(), calls=%async_computation.20 | async-start | bytes 3538944 | tf_op jit(solution)/shard_map/psum | solution.py:207
  657.9 462.2 %copy-start.6 = (f32[1024,768]{1,0:T(8,128)S(1)}, f32[1024,768]{1,0:T(8,128)}, u32[]{:S(2)}) copy-start(f32[1024,768]{1,0:T(8,128)} %copy-done.5) | copy-start | bytes 9437188
  1120.1 69.7 %copy-start.29 = (f32[96,12]{0,1:T(8,128)S(1)}, f32[96,12]{0,1:T(8,128)}, u32[]{:S(2)}) copy-start(f32[96,12]{0,1:T(8,128)} %param.27) | copy-start | bytes 13828
  1120.1 69.7 %copy-start.32 = (f32[96,12]{0,1:T(8,128)S(1)}, f32[96,12]{0,1:T(8,128)}, u32[]{:S(2)}) copy-start(f32[96,12]{0,1:T(8,128)} %param.37) | copy-start | bytes 13828
  1120.1 69.7 %copy-start.33 = (f32[96,12]{0,1:T(8,128)S(1)}, f32[96,12]{0,1:T(8,128)}, u32[]{:S(2)}) copy-start(f32[96,12]{0,1:T(8,128)} %param.32) | copy-start | bytes 13828
  1120.1 112.5 %copy-start.21 = (f32[96,768]{1,0:T(8,128)S(1)}, f32[96,768]{1,0:T(8,128)}, u32[]{:S(2)}) copy-start(f32[96,768]{1,0:T(8,128)} %param.24) | copy-start | bytes 884740
  1234.9 4.0 copy-start.12
  1234.9 4.0 copy-start.16
  1234.9 4.0 copy-start.17
  1234.9 4.0 copy-start.23
  1238.9 2.6 copy-start.13
  1238.9 2.6 copy-start.18
  1238.9 3.5 copy-start.19
  1239.0 3.6 copy-start.22
  (3 other events, 4.2 us)
Sparse Core Ops, SparseCore 0:
  10.8 67.3 all-gather.7
  89.5 45.0 all-gather.11
  136.8 46.3 all-gather.9
  185.8 41.1 all-gather.13
  229.5 77.9 all-gather.15
  310.2 77.6 all-gather.17
  464.4 57.2 reduce-scatter.13
  524.2 58.8 reduce-scatter.11
  586.6 69.6 reduce-scatter.15
  659.7 161.2 reduce-scatter.17
  824.7 161.2 reduce-scatter.19
  989.4 128.6 reduce-scatter.21
  1121.9 61.3 reduce-scatter.23
  1187.5 45.1 all-reduce.2
where the time goes:
time: 1260 us; the launch traced here: 1250 us
  waiting for transfers between devices  843 us (67%)
  matrix products  210 us (17%)
  local copies, waits for them, and re-layouts  74.5 us (6%)
  other arithmetic  71.6 us (6%)
  blocking collectives  36.3 us (3%)
  between operations  15.5 us (1%)
    reduce_scatter x1, waiting for transfers between devices, local(): lax.psum_scatter(gw_up, 'tab', scatter_dimension=0, tiled=True)  163 us
    reduce_scatter x1, waiting for transfers between devices, local(): lax.psum_scatter(gw_down, 'tab', scatter_dimension=0, tiled=True)  163 us
    reduce_scatter x1, waiting for transfers between devices, local(): lax.psum_scatter(gw_qkv, 'tab', scatter_dimension=0, tiled=True)  130 us
    all_gather x1, waiting for transfers between devices, local(): lax.all_gather(w_up.astype(jnp.bfloat16), 'tab', axis=0, tiled=True)  76.3 us
    all_gather x1, waiting for transfers between devices, local(): lax.all_gather(w_qkv.astype(jnp.bfloat16), 'tab', axis=0, tiled=True)  68.8 us
    unnamed x15, waiting for transfers between devices  54.1 us
    reduce_scatter x1, waiting for transfers between devices, local(): lax.psum_scatter(gw_out, 'tab', scatter_dimension=0, tiled=True)  45.1 us
    all_gather x1, waiting for transfers between devices, local(): lax.all_gather(w_down.astype(jnp.bfloat16), 'tab', axis=0, tiled=True)  44.3 us
  transfers between devices with their start and end apart: 14, of which 13 were waited for; matrix products, arithmetic and copies ran while one was open for 20% of the time, Pallas kernels for 0%

commit v1 on v0

--- a/solution.py
+++ b/solution.py
@@ -1,8 +1,10 @@
+import functools
 from functools import partial
 import jax
 import jax.numpy as jnp
 from jax import lax
 from jax.sharding import PartitionSpec as P
+from jax.lax import axis_index, axis_size, ppermute
 
 D = 768
 H = 12
@@ -15,6 +17,31 @@
 ADAM_EPS = 1e-08
 DECAY = 0.01
 RATES = (1.0, 15.0, 1.0, 0.5, 5.0)
+
+
+def supply_all_the_sheets(local_values, in_dim):
+    left_arr = axis_size("tab")
+    e_next, wide_out, later = (left_arr, axis_index("tab"), local_values.shape[in_dim])
+    arrivals = [j * e_next if no == in_dim else j for no, j in enumerate(local_values.shape)]
+    found_now = jnp.zeros(arrivals, local_values.dtype)
+    response = z2 = local_values
+    after = lax.dynamic_update_slice_in_dim(found_now, local_values, wide_out * later, axis=in_dim)
+    for idx in [*range(1, e_next // 2 + 1)]:
+        response = ppermute(
+            response, axis_name="tab", perm=[(no, (no + 1) % e_next) for no in range(e_next)]
+        )
+        after = lax.dynamic_update_slice_in_dim(
+            after, response, (wide_out - idx) % e_next * later, axis=in_dim
+        )
+        if 2 * idx < e_next:
+            z2 = ppermute(z2, "tab", [(no, (no - 1) % e_next) for no in range(e_next)])
+            after = lax.dynamic_update_slice_in_dim(
+                after, z2, (wide_out + idx) % e_next * later, axis=in_dim
+            )
+    return after
+
+
+view_the_block = functools.partial(supply_all_the_sheets, in_dim=0)
 
 
 def layer_norm(hidden, gain_vec, shift_vec):
@@ -71,7 +98,7 @@
     firsts = (first_qkv, first_out, first_up, first_down, first_vec)
     seconds = (second_qkv, second_out, second_up, second_down, second_vec)
     full_qkv, full_out, full_up, full_down, full_vec = (
-        lax.all_gather(w_qkv.astype(jnp.bfloat16), "tab", axis=0, tiled=True),
+        view_the_block(w_qkv.astype(jnp.bfloat16)),
         lax.all_gather(w_out.astype(jnp.bfloat16), "tab", axis=0, tiled=True),
         lax.all_gather(w_up.astype(jnp.bfloat16), "tab", axis=0, tiled=True),
         lax.all_gather(w_down.astype(jnp.bfloat16), "tab", axis=0, tiled=True),

time: 1260 us -> 1270 us (level)
  starting transfers between devices: 1.22 us -> 20.9 us
  waiting for transfers between devices: 843 us -> 824 us
    all_gather x1 -> x0, waiting for transfers between devices: 68.8 us -> none  [local(): lax.all_gather(w_qkv.astype(jnp.bfloat16), 'tab', axis=0, tiled=True)]
    ppermute x0 -> x7, waiting for transfers between devices: none -> 51.2 us  [the longest x4 51.2 us: supply_all_the_sheets(): ppermute(response, axis_name='tab', perm=[(no, (no + 1) % e_next) for no...]
    ppermute x0 -> x7, starting transfers between devices: none -> 19.5 us  [the longest x4 10.4 us: supply_all_the_sheets(): ppermute(response, axis_name='tab', perm=[(no, (no + 1) % e_next) for no...]
    unnamed x80 -> x86, local copies, waits for them, and re-layouts: 25.7 us -> 28.4 us
    unnamed x15 -> x14, waiting for transfers between devices: 54.1 us -> 53.9 us
  transfers between devices with their start and end apart: 14 -> 20, of which waited for: 13 -> 16; matrix products, arithmetic and copies ran while one was open for 20% -> 20% of each run, Pallas kernels for 0% -> 0%
where the time goes in v1:
time: 1270 us; the launch traced here: 1260 us
  waiting for transfers between devices  824 us (65%)
  matrix products  210 us (17%)
  local copies, waits for them, and re-layouts  83 us (7%)
  other arithmetic  69.7 us (5%)
  blocking collectives  36.3 us (3%)
  starting transfers between devices  20.9 us (2%)
  between operations  15.5 us (1%)
    reduce_scatter x1, waiting for transfers between devices, local(): lax.psum_scatter(gw_up, 'tab', scatter_dimension=0, tiled=True)  163 us
    reduce_scatter x1, waiting for transfers between devices, local(): lax.psum_scatter(gw_down, 'tab', scatter_dimension=0, tiled=True)  163 us
    reduce_scatter x1, waiting for transfers between devices, local(): lax.psum_scatter(gw_qkv, 'tab', scatter_dimension=0, tiled=True)  130 us
    all_gather x1, waiting for transfers between devices, local(): lax.all_gather(w_up.astype(jnp.bfloat16), 'tab', axis=0, tiled=True)  76.3 us
    unnamed x14, waiting for transfers between devices  53.9 us
    ppermute x4, waiting for transfers between devices, supply_all_the_sheets(): ppermute(response, axis_name='tab', perm=[(no, (no + 1) % e_next) for no...  51.2 us
    reduce_scatter x1, waiting for transfers between devices, local(): lax.psum_scatter(gw_out, 'tab', scatter_dimension=0, tiled=True)  45 us
    all_gather x1, waiting for transfers between devices, local(): lax.all_gather(w_down.astype(jnp.bfloat16), 'tab', axis=0, tiled=True)  44 us
  transfers between devices with their start and end apart: 20, of which 16 were waited for; matrix products, arithmetic and copies ran while one was open for 20% of the time, Pallas kernels for 0%

profile of v1, /device:TPU:0, one launch (start us, length us, event | category | flops | bytes accessed | tf_op | source)
XLA Modules:
  0.0 1259.6 jit_solution(17961977750830140269)
XLA Ops:
  16.3 15.9 %collective-permute-done = bf16[96,2304]{1,0:T(8,128)(2,1)S(1)} collective-permute-done((bf16[96,2304]{1,0:T(8,128)(2,1)S(1)}, bf16[96,2304]{1,0:T(8,128)(2,1)S(1)}, u32[]{:S(2)}, u32[]{:S(2)}) %collective-permute-start) | collective-permute-done | bytes 442400 | tf_op jit(solution)/shard_map/ppermute | solution.py:30
  34.6 3.0 collective-permute-start.3
  39.3 13.4 %collective-permute-done.2 = bf16[96,2304]{1,0:T(8,128)(2,1)S(1)} collective-permute-done((bf16[96,2304]{1,0:T(8,128)(2,1)S(1)}, bf16[96,2304]{1,0:T(8,128)(2,1)S(1)}, u32[]{:S(2)}, u32[]{:S(2)}) %collective-permute-start.2) | collective-permute-done | bytes 442400 | tf_op jit(solution)/shard_map/ppermute | solution.py:30
  55.2 3.0 collective-permute-start.5
  59.8 12.7 %collective-permute-done.4 = bf16[96,2304]{1,0:T(8,128)(2,1)S(1)} collective-permute-done((bf16[96,2304]{1,0:T(8,128)(2,1)S(1)}, bf16[96,2304]{1,0:T(8,128)(2,1)S(1)}, u32[]{:S(2)}, u32[]{:S(2)}) %collective-permute-start.4) | collective-permute-done | bytes 442400 | tf_op jit(solution)/shard_map/ppermute | solution.py:30
  76.6 9.2 collective-permute-done.6
  86.6 5.8 convolution_bitcast_fusion
  92.5 3.6 copy-done.9
  97.5 30.6 %all-gather = bf16[8,96,12]{1,2,0:T(8,128)(2,1)S(1)} all-gather(bf16[1,96,12]{1,2,0:T(8,128)(2,1)S(1)} %convert_bitcast_fusion), channel_id=1, replica_groups=mesh['tab'=8,'blk'=4] {'tab'}, dimensions={0}, use_global_device_ids=true | all-gather | bytes 20736 | tf_op jit(solution)/shard_map/all_gather | solution.py:105
  128.8 4.7 fusion.16
  139.1 3.3 all-gather.9.cloned.1.call-done
  142.5 8.6 copy.104
  151.1 12.9 %fusion.12 = (f32[8,12,128]{2,1,0:T(8,128)S(1)}, f32[8,12,128,512]{3,2,1,0:T(8,128)}) fusion(pred[8,512]{1,0:T(8,128)(4,1)S(1)} %iota_compare_fusion, bf16[8,512,12,64]{1,3,2,0:T(8,128)(2,1)} %bitcast.96, bf16[8,128,12,64]{1,0,3,2:T(8,128)(2,1)S(1)} %bitcast.101), kind=kOutput, calls=%fused_computation.29 | convolution fusion | flops 824168448 | bytes 33083392 | tf_op jit(solution)/shard_map/bqhd,bkhd->bhqk/dot_general | solution.py:118
  164.0 11.6 fusion
  176.3 14.7 %all-gather.7.cloned.1.call-done = bf16[8,512,768]{2,1,0:T(8,128)(2,1)} async-done(((bf16[8,128,768]{2,1,0:T(8,128)(2,1)}), bf16[8,512,768]{2,1,0:T(8,128)(2,1)}) %all-gather.7.cloned.1.call-update) | async-done | bytes 6291472 | tf_op jit(solution)/shard_map/all_gather | solution.py:132
  191.0 8.6 copy.102
  199.6 13.4 %fusion.35 = bf16[8,128,12,64]{1,3,2,0:T(8,128)(2,1)S(1)} fusion(bf16[8,512,12,64]{1,3,2,0:T(8,128)(2,1)} %bitcast.99, f32[8,12,128]{2,1,0:T(8,128)S(1)} %fusion, f32[8,12,128]{2,1,0:T(8,128)S(1)} %get-tuple-element.138, f32[8,12,128,512]{3,2,1,0:T(8,128)} %get-tuple-element.139, pred[8,512]{1,0:T(8,128)(4,1)S(1)} %iota_compare_fusion), kind=kOutput, calls=%fused_computation.80 | convolution fusion | flops 837550080 | bytes 33132544 | tf_op jit(solution)/shard_map/bhqk,bkhd->bqhd/dot_general | solution.py:143
  215.5 19.5 %all-gather.11.cloned.1.call-done = bf16[768,768]{1,0:T(8,128)(2,1)} async-done(((bf16[96,768]{1,0:T(8,128)(2,1)}), bf16[768,768]{1,0:T(8,128)(2,1)}) %all-gather.11.cloned.1.call-update) | async-done | bytes 1179664 | tf_op jit(solution)/shard_map/all_gather | solution.py:102
  234.9 3.9 fusion.84
  239.3 76.3 %all-gather.13.cloned.1.call-done = bf16[768,3072]{1,0:T(8,128)(2,1)} async-done(((bf16[96,3072]{1,0:T(8,128)(2,1)}), bf16[768,3072]{1,0:T(8,128)(2,1)}) %all-gather.13.cloned.1.call-update) | async-done | bytes 4718608 | tf_op jit(solution)/shard_map/all_gather | solution.py:103
  315.6 36.3 %multiply_convert_fusion.2 = (bf16[1024,3072]{1,0:T(8,128)(2,1)}, f32[1024,3072]{1,0:T(8,128)}, f32[1024,3072]{1,0:T(8,128)}) fusion(f32[3072]{0:T(1024)S(1)} %add.300, bf16[768,3072]{1,0:T(8,128)(2,1)} %all-gather.13.cloned.1.call-done, f32[1024,768]{1,0:T(8,128)S(1)} %get-tuple-element.141, f32[768]{0:T(1024)S(1)} %get-tuple-element.96, ...), kind=kOutput, calls=%fused_computation.14 | convolution fusion | flops 5043388416 | bytes 39348224 | tf_op jit(solution)/shard_map/dot_general | solution.py:152
  351.9 44.0 %all-gather.15.cloned.1.call-done = bf16[3072,768]{1,0:T(8,128)(2,1)} async-done(((bf16[384,768]{1,0:T(8,128)(2,1)}), bf16[3072,768]{1,0:T(8,128)(2,1)}) %all-gather.15.cloned.1.call-update) | async-done | bytes 4718608 | tf_op jit(solution)/shard_map/all_gather | solution.py:104
  395.9 8.8 fusion.85
  407.9 3.1 fusion.82
  411.0 19.0 %fusion.86 = (f32[3072]{0:T(1024)S(1)}, bf16[1024,3072]{1,0:T(8,128)(2,1)}) fusion(f32[1024,3072]{1,0:T(8,128)} %get-tuple-element.130, bf16[3072,768]{1,0:T(8,128)(2,1)} %all-gather.15.cloned.1.call-done, f32[1024,768]{1,0:T(8,128)} %get-tuple-element.128, f32[1024]{0:T(1024)S(1)} %negate_multiply_fusion.2, f32[1024,3072]{1,0:T(8,128)} %get-tuple-element.142, ...), kind=kOutput, calls=%fused_computation.160 | convolution fusion | flops 4883739648 | bytes 39350272 | tf_op jit(solution)/shard_map/dot_general | solution.py:61
  430.0 10.0 multiply_reduce_fusion.1
  450.3 13.1 %fusion.13 = bf16[8,12,64,512]{3,2,1,0:T(8,128)(2,1)} fusion(f32[8,12,128]{2,1,0:T(8,128)S(1)} %copy-done.26, f32[8,12,128,512]{3,2,1,0:T(8,128)} %get-tuple-element.139, pred[8,512]{1,0:T(8,128)(4,1)S(1)} %copy-done.28, bf16[8,128,12,64]{1,0,3,2:T(8,128)(2,1)S(1)} %bitcast.110), kind=kOutput, calls=%fused_computation.35 | convolution fusion | flops 833617920 | bytes 33083392 | tf_op jit(solution)/shard_map/bhqk,bqhd->bkhd/dot_general | solution.py:199
  463.4 8.7 copy.113
  472.1 24.2 %multiply_reduce_fusion = (f32[8,12,128]{2,1,0:T(8,128)S(1)}, f32[8,12,128,512]{3,2,1,0:T(8,128)}) fusion(f32[8,12,128]{2,1,0:T(8,128)S(1)} %copy-done.26, f32[8,12,128,512]{3,2,1,0:T(8,128)} %get-tuple-element.139, pred[8,512]{1,0:T(8,128)(4,1)S(1)} %copy-done.28, bf16[8,512,12,64]{1,3,2,0:T(8,128)(2,1)} %bitcast.100, bf16[8,128,12,64]{1,0,3,2:T(8,128)(2,1)} %bitcast.111), kind=kOutput, calls=%fused_computation.1 | convolution fusion | flops 836751360 | bytes 58298368 | tf_op jit(solution)/shard_map/bqhd,bkhd->bhqk/dot_general | solution.py:181
  496.3 17.0 %multiply_convert_fusion = bf16[8,12,128,512]{3,2,1,0:T(8,128)(2,1)S(1)} fusion(f32[8,12,128,512]{3,2,1,0:T(8,128)} %get-tuple-element.147, f32[8,12,128]{2,1,0:T(8,128)S(1)} %get-tuple-element.146, f32[8,12,128]{2,1,0:T(8,128)S(1)} %copy-done.26, f32[8,12,128,512]{3,2,1,0:T(8,128)} %get-tuple-element.139, pred[8,512]{1,0:T(8,128)(4,1)S(1)} %copy-done.28), kind=kLoop, calls=%fused_computation | loop fusion | flops 37748736 | bytes 63016960 | tf_op jit(solution)/shard_map/convert_element_type | solution.py:185
  513.3 4.2 multiply_convert_fusion.1
  519.8 8.7 copy.111
  528.5 5.4 fusion.32
  534.0 10.8 fusion.22
  546.8 10.8 fusion.62
  558.0 10.8 multiply_reduce_fusion.5
  572.9 18.0 %reduce-scatter.12.cloned.1.call-done = bf16[8,128,768]{2,1,0:T(8,128)(2,1)} async-done(((bf16[8,512,768]{2,1,0:T(8,128)(2,1)}), bf16[8,128,768]{2,1,0:T(8,128)(2,1)}) %reduce-scatter.12.cloned.1.call-update) | async-done | bytes 1572880 | tf_op jit(solution)/shard_map/reduce_scatter | solution.py:203
  593.5 8.7 convolution_bitcast_fusion.1
  602.2 8.0 copy.117
  618.9 45.0 %reduce-scatter.16.cloned.1.call-done = f32[96,768]{1,0:T(8,128)} async-done(((f32[768,768]{1,0:T(8,128)}), f32[96,768]{1,0:T(8,128)}) %reduce-scatter.16.cloned.1.call-update) | async-done | bytes 294928 | tf_op jit(solution)/shard_map/reduce_scatter | solution.py:228
  665.6 163.4 %reduce-scatter.18.cloned.1.call-done = f32[96,3072]{1,0:T(8,128)} async-done(((f32[768,3072]{1,0:T(8,128)}), f32[96,3072]{1,0:T(8,128)}) %reduce-scatter.18.cloned.1.call-update) | async-done | bytes 1179664 | tf_op jit(solution)/shard_map/reduce_scatter | solution.py:229
  831.1 162.6 %reduce-scatter.20.cloned.1.call-done = f32[384,768]{1,0:T(8,128)} async-done(((f32[3072,768]{1,0:T(8,128)}), f32[384,768]{1,0:T(8,128)}) %reduce-scatter.20.cloned.1.call-update) | async-done | bytes 1179664 | tf_op jit(solution)/shard_map/reduce_scatter | solution.py:230
  995.8 130.2 %reduce-scatter.22.cloned.1.call-done = f32[96,2304]{1,0:T(8,128)} async-done(((f32[768,2304]{1,0:T(8,128)}), f32[96,2304]{1,0:T(8,128)}) %reduce-scatter.22.cloned.1.call-update) | async-done | bytes 884752 | tf_op jit(solution)/shard_map/reduce_scatter | solution.py:227
  1128.0 9.3 add_add_fusion.4
  1137.3 53.7 %reduce-scatter.24.cloned.1.call-done = f32[96,12]{1,0:T(8,128)} async-done(((f32[768,12]{1,0:T(8,128)}), f32[96,12]{1,0:T(8,128)}) %reduce-scatter.24.cloned.1.call-update) | async-done | bytes 4624
  1191.8 5.7 psum.39
  1198.2 42.3 %all-reduce.3.cloned.1.call-done = (bf16[96,2304]{1,0:T(8,128)(2,1)}, bf16[96,768]{1,0:T(8,128)(2,1)}, bf16[96,3072]{1,0:T(8,128)(2,1)}, bf16[384,768]{1,0:T(8,128)(2,1)}) async-done(((bf16[96,2304]{1,0:T(8,128)(2,1)}, bf16[96,768]{1,0:T(8,128)(2,1)}, bf16[96,3072]{1,0:T(8,128)(2,1)}, bf16[384,768]{1,0:T(8,128)(2,1)}), (bf16[96,2304]{1,0:T(8,128)(2,1)}, bf16[96,768]{1,0:T(8,128)(2,1)}, ...) | async-done | bytes 1769488 | tf_op jit(solution)/shard_map/psum | solution.py:234
  1242.7 4.0 fusion.78
  (181 shorter events, 83.7 us)
Async XLA Ops:
  7.2 135.3 %all-gather.9.cloned.1.call-start = ((), (), s32[]{:S(2)}) async-start(), calls=%async_computation.8 | async-start | bytes 7864320 | tf_op jit(solution)/shard_map/all_gather | solution.py:131
  10.3 21.9 %collective-permute-start = (bf16[96,2304]{1,0:T(8,128)(2,1)S(1)}, bf16[96,2304]{1,0:T(8,128)(2,1)S(1)}, u32[]{:S(2)}, u32[]{:S(2)}) collective-permute-start(bf16[96,2304]{1,0:T(8,128)(2,1)S(1)} %get-tuple-element.132), channel_id=1, source_target_pairs={{0,4},{4,8},{8,12},{12,16},{16,20},{20,24},{24,28},{28,0},{1,5},{5... | collective-permute-start | bytes 1327112 | tf_op jit(solution)/shard_map/ppermute | solution.py:30
  13.3 21.4 %collective-permute-start.1 = (bf16[96,2304]{1,0:T(8,128)(2,1)S(1)}, bf16[96,2304]{1,0:T(8,128)(2,1)S(1)}, u32[]{:S(2)}, u32[]{:S(2)}) collective-permute-start(bf16[96,2304]{1,0:T(8,128)(2,1)S(1)} %get-tuple-element.132), channel_id=1, source_target_pairs={{0,28},{4,0},{8,4},{12,8},{16,12},{20,16},{24,20},{28,24},{1,29},{... | collective-permute-start | bytes 1327112 | tf_op jit(solution)/shard_map/ppermute | solution.py:37
  16.3 70.3 %copy-start.38 = (bf16[8,128,768]{2,1,0:T(8,128)(2,1)S(1)}, bf16[8,128,768]{2,1,0:T(8,128)(2,1)}, u32[]{:S(2)}) copy-start(bf16[8,128,768]{2,1,0:T(8,128)(2,1)} %param.19) | copy-start | bytes 4718596
  32.2 20.5 %collective-permute-start.2 = (bf16[96,2304]{1,0:T(8,128)(2,1)S(1)}, bf16[96,2304]{1,0:T(8,128)(2,1)S(1)}, u32[]{:S(2)}, u32[]{:S(2)}) collective-permute-start(bf16[96,2304]{1,0:T(8,128)(2,1)S(1)} %collective-permute-done), channel_id=1, source_target_pairs={{0,4},{4,8},{8,12},{12,16},{16,20},{20,24},{24,28},{28,0},{1,5},{5... | collective-permute-start | bytes 1327112 | tf_op jit(solution)/shard_map/ppermute | solution.py:30
  34.6 20.5 %collective-permute-start.3 = (bf16[96,2304]{1,0:T(8,128)(2,1)S(1)}, bf16[96,2304]{1,0:T(8,128)(2,1)S(1)}, u32[]{:S(2)}, u32[]{:S(2)}) collective-permute-start(bf16[96,2304]{1,0:T(8,128)(2,1)S(1)} %collective-permute-done.1), channel_id=1, source_target_pairs={{0,28},{4,0},{8,4},{12,8},{16,12},{20,16},{24,20},{28,24},{1,29},{... | collective-permute-start | bytes 1327112 | tf_op jit(solution)/shard_map/ppermute | solution.py:37
  52.7 19.8 %collective-permute-start.4 = (bf16[96,2304]{1,0:T(8,128)(2,1)S(1)}, bf16[96,2304]{1,0:T(8,128)(2,1)S(1)}, u32[]{:S(2)}, u32[]{:S(2)}) collective-permute-start(bf16[96,2304]{1,0:T(8,128)(2,1)S(1)} %collective-permute-done.2), channel_id=1, source_target_pairs={{0,4},{4,8},{8,12},{12,16},{16,20},{20,24},{24,28},{28,0},{1,5},{5... | collective-permute-start | bytes 1327112 | tf_op jit(solution)/shard_map/ppermute | solution.py:30
  55.2 20.6 %collective-permute-start.5 = (bf16[96,2304]{1,0:T(8,128)(2,1)S(1)}, bf16[96,2304]{1,0:T(8,128)(2,1)S(1)}, u32[]{:S(2)}, u32[]{:S(2)}) collective-permute-start(bf16[96,2304]{1,0:T(8,128)(2,1)S(1)} %collective-permute-done.3), channel_id=1, source_target_pairs={{0,28},{4,0},{8,4},{12,8},{16,12},{20,16},{24,20},{28,24},{1,29},{... | collective-permute-start | bytes 1327112 | tf_op jit(solution)/shard_map/ppermute | solution.py:37
  72.5 13.3 %collective-permute-start.6 = (bf16[96,2304]{1,0:T(8,128)(2,1)S(1)}, bf16[96,2304]{1,0:T(8,128)(2,1)S(1)}, u32[]{:S(2)}, u32[]{:S(2)}) collective-permute-start(bf16[96,2304]{1,0:T(8,128)(2,1)S(1)} %collective-permute-done.4), channel_id=1, source_target_pairs={{0,4},{4,8},{8,12},{12,16},{16,20},{20,24},{24,28},{28,0},{1,5},{5... | collective-permute-start | bytes 1327112 | tf_op jit(solution)/shard_map/ppermute | solution.py:30
  92.5 3.6 copy-start.9
  97.4 93.6 %all-gather.7.cloned.1.call-start = ((), (), s32[]{:S(2)}) async-start(), calls=%async_computation.7 | async-start | bytes 7864320 | tf_op jit(solution)/shard_map/all_gather | solution.py:132
  128.8 4.7 copy-start.22
  128.8 5.5 copy-start.11
  133.5 4.3 copy-start.37
  133.5 101.4 %all-gather.11.cloned.1.call-start = ((), (), s32[]{:S(2)}) async-start(), calls=%async_computation.9 | async-start | bytes 1327104 | tf_op jit(solution)/shard_map/all_gather | solution.py:102
  134.3 181.3 %all-gather.13.cloned.1.call-start = ((), (), s32[]{:S(2)}) async-start(), calls=%async_computation.10 | async-start | bytes 5308416 | tf_op jit(solution)/shard_map/all_gather | solution.py:103
  135.2 260.7 %all-gather.15.cloned.1.call-start = ((), (), s32[]{:S(2)}) async-start(), calls=%async_computation.11 | async-start | bytes 5308416 | tf_op jit(solution)/shard_map/all_gather | solution.py:104
  137.5 433.1 %reduce-scatter.14.cloned.1.call-start = ((), (), s32[]{:S(2)}) async-start(), calls=%async_computation.13 | async-start | bytes 7864320 | tf_op jit(solution)/shard_map/reduce_scatter | solution.py:206
  137.9 61.7 %copy-start.27 = (pred[8,512]{1,0:T(8,128)(4,1)}, pred[8,512]{1,0:T(8,128)(4,1)S(1)}, u32[]{:S(2)}) copy-start(pred[8,512]{1,0:T(8,128)(4,1)S(1)} %iota_compare_fusion) | copy-start | bytes 12292
  139.1 12.0 copy-start.1
  315.6 80.3 %copy-start.36 = (f32[768]{0:T(1024)S(1)}, f32[768]{0:T(1024)}, u32[]{:S(2)}) copy-start(f32[768]{0:T(1024)} %get-tuple-element.95) | copy-start | bytes 9220
  440.0 3.1 copy-start.39
  445.8 4.5 copy-start.26
  445.8 4.5 copy-start.28
  450.2 13.1 %copy-start.10 = (bf16[96,8,8,128]{3,2,1,0:T(8,128)(2,1)}, bf16[96,8,8,128]{3,2,1,0:T(8,128)(2,1)S(1)}, u32[]{:S(2)}) copy-start(bf16[96,8,8,128]{3,2,1,0:T(8,128)(2,1)S(1)} %copy.123) | copy-start | bytes 4718596
  472.1 118.8 %reduce-scatter.12.cloned.1.call-start = ((), (), s32[]{:S(2)}) async-start(), calls=%async_computation.12 | async-start | bytes 7864320 | tf_op jit(solution)/shard_map/reduce_scatter | solution.py:203
  496.3 17.1 %copy-start.2 = (bf16[96,8,8,128]{3,2,1,0:T(8,128)(2,1)S(1)}, bf16[96,8,8,128]{3,2,1,0:T(8,128)(2,1)}, u32[]{:S(2)}) copy-start(bf16[96,8,8,128]{3,2,1,0:T(8,128)(2,1)} %copy-done.1) | copy-start | bytes 4718596
  513.3 6.4 copy-start
  528.5 135.5 %reduce-scatter.16.cloned.1.call-start = ((), (), s32[]{:S(2)}) async-start(), calls=%async_computation.14 | async-start | bytes 2654208 | tf_op jit(solution)/shard_map/reduce_scatter | solution.py:228
  533.9 295.0 %reduce-scatter.18.cloned.1.call-start = ((), (), s32[]{:S(2)}) async-start(), calls=%async_computation.15 | async-start | bytes 10616832 | tf_op jit(solution)/shard_map/reduce_scatter | solution.py:229
  544.8 448.9 %reduce-scatter.20.cloned.1.call-start = ((), (), s32[]{:S(2)}) async-start(), calls=%async_computation.16 | async-start | bytes 10616832 | tf_op jit(solution)/shard_map/reduce_scatter | solution.py:230
  557.6 568.4 %reduce-scatter.22.cloned.1.call-start = ((), (), s32[]{:S(2)}) async-start(), calls=%async_computation.17 | async-start | bytes 7962624 | tf_op jit(solution)/shard_map/reduce_scatter | solution.py:227
  570.6 23.0 %copy-start.16 = (bf16[96,8,8,128]{3,1,2,0:T(8,128)(2,1)}, bf16[96,8,8,128]{3,1,2,0:T(8,128)(2,1)S(1)}, u32[]{:S(2)}) copy-start(bf16[96,8,8,128]{3,1,2,0:T(8,128)(2,1)S(1)} %copy.149) | copy-start | bytes 4718596
  572.9 29.3 %copy-start.17 = (bf16[1024,768]{0,1:T(8,128)(2,1)}, bf16[1024,768]{0,1:T(8,128)(2,1)S(1)}, u32[]{:S(2)}) copy-start(bf16[1024,768]{0,1:T(8,128)(2,1)S(1)} %copy.115) | copy-start | bytes 4718596
  610.3 580.7 %reduce-scatter.24.cloned.1.call-start = ((), (), s32[]{:S(2)}) async-start(), calls=%async_computation.18 | async-start | bytes 442368
  612.0 2.9 copy-start.8
  618.0 622.5 %all-reduce.3.cloned.1.call-start = ((), (), s32[]{:S(2)}) async-start(), calls=%async_computation.19 | async-start | bytes 3538944 | tf_op jit(solution)/shard_map/psum | solution.py:234
  665.6 462.4 %copy-start.6 = (f32[1024,768]{1,0:T(8,128)S(1)}, f32[1024,768]{1,0:T(8,128)}, u32[]{:S(2)}) copy-start(f32[1024,768]{1,0:T(8,128)} %copy-done.5) | copy-start | bytes 9437188
  1128.0 69.5 %copy-start.31 = (f32[96,12]{0,1:T(8,128)S(1)}, f32[96,12]{0,1:T(8,128)}, u32[]{:S(2)}) copy-start(f32[96,12]{0,1:T(8,128)} %param.27) | copy-start | bytes 13828
  1128.0 69.5 %copy-start.34 = (f32[96,12]{0,1:T(8,128)S(1)}, f32[96,12]{0,1:T(8,128)}, u32[]{:S(2)}) copy-start(f32[96,12]{0,1:T(8,128)} %param.37) | copy-start | bytes 13828
  1128.0 69.5 %copy-start.35 = (f32[96,12]{0,1:T(8,128)S(1)}, f32[96,12]{0,1:T(8,128)}, u32[]{:S(2)}) copy-start(f32[96,12]{0,1:T(8,128)} %param.32) | copy-start | bytes 13828
  1128.0 112.4 %copy-start.23 = (f32[96,768]{1,0:T(8,128)S(1)}, f32[96,768]{1,0:T(8,128)}, u32[]{:S(2)}) copy-start(f32[96,768]{1,0:T(8,128)} %param.24) | copy-start | bytes 884740
  1242.7 4.0 copy-start.12
  1242.7 4.0 copy-start.18
  1242.7 4.0 copy-start.19
  1242.7 4.0 copy-start.25
  1246.8 3.5 copy-start.21
  1246.8 3.6 copy-start.24
  (12 other events, 21.8 us)
Sparse Core Ops, SparseCore 0:
  97.5 44.8 all-gather.8
  144.6 46.3 all-gather.6
  193.8 41.1 all-gather.10
  237.5 77.9 all-gather.12
  318.2 77.6 all-gather.14
  472.2 57.2 reduce-scatter.13
  532.0 58.8 reduce-scatter.11
  594.4 69.5 reduce-scatter.15
  667.5 161.3 reduce-scatter.17
  832.4 161.2 reduce-scatter.19
  997.4 128.5 reduce-scatter.21
  1129.7 61.2 reduce-scatter.23
  1195.3 45.1 all-reduce.2
